TPU v7x, 32 devices: a whole 2x2x4 slice. The times are simulated.
32 devices in a mesh: grp: 4 (over z), dom: 8 (over y, x, core).
Axes of the slice: x: 2, y: 2, z: 4, core: 2. Of those that a mesh axis runs over, the one named last changes fastest.
Arguments:
- operator_blocks: float32 [128, 16, 4096], P(('grp', 'dom')), may hold values from -0.75 to 0.75
- operator_cols: int32 [128, 16], P(('grp', 'dom')), may hold values from 0 to 15, as said below
- halo_count: int32 [128], P(('grp', 'dom')), may hold values from 2 to 4, as said below
- prolong_blocks: float32 [128, 8, 4096], P(('grp', 'dom')), may hold values from -0.75 to 0.75
- prolong_cols: int32 [128, 8], P(('grp', 'dom')), may hold values from 0 to 63, as said below
- prolong_slot: int32 [128, 8], P(('grp', 'dom')), may hold values from 0 to 15, as said below
- send_lists: int32 [32, 8], P(('grp', 'dom')), may hold values from 0 to 3
- slot_owner_row: int32 [32, 16], P(('grp', 'dom')), may hold values from 0 to 2, as said below
- coarse_pattern: int32 [64, 16], P(('grp', 'dom')), may hold values from 0 to 63, as said below
Outputs:
- coarse_blocks: float32 [64, 16, 4096], P(('grp', 'dom'))
Inputs may be any that keep to these rules, and one draw needn't show every extreme that they name: `operator_cols`: slots below 12 hold values below 16, the others values below 8. Slots at or beyond a row's live count hold valid values whose blocks do not count. `halo_count`: the first fine row of every device has 4. `prolong_cols`: the 8 values of a row are different. A row on grp index g names coarse rows owned by devices of grp index g only. Slot t of device v stands for owner dom index t // 2 and owner coarse row slot_owner_row[v, t]; prolong_cols[i, j] = ((v // 8) * 8 + s // 2) * 2 + slot_owner_row[v, s] for s = prolong_slot[i, j]; the slots of a row are different and never empty. `slot_owner_row`: the value 2 marks an empty slot; the live values of one device for one owner are different; every device fills all 2 slots of its own dom index and the first slot of every owner, and no other slot. `coarse_pattern`: the 16 values of a row are different.
All inputs are finite; a program needn't handle non-finite values.
Results may differ from a plain program's by a relative error of at most 0.0003.
Values sent between devices are 32-bit elements; how exact they have to be, the bound alone decides.
A program may use at most 128 MiB of HBM per device.

v0:
```python
import functools

import jax
import jax.numpy as jnp
from jax import lax
from jax.experimental import pallas as pl
from jax.experimental.pallas import tpu as pltpu
from jax.sharding import PartitionSpec as P

BS = 64
KG = 12
KH = 4
LANES = 128


def any_spec():
    return pl.BlockSpec(memory_space=pl.ANY)


def vmem_spec():
    return pl.BlockSpec(memory_space=pltpu.VMEM)


def smem_spec():
    return pl.BlockSpec(memory_space=pltpu.SMEM)


def gather_kernel(
    n_grp, n_dom, rows, hs,
    panels, outgoing, dom_meta, grp_meta,
    table, meta,
    own_sem, line_send, line_recv, dom_send, dom_recv, meta_send, meta_recv,
):
    g = lax.axis_index("grp")
    me = lax.axis_index("dom")
    far_base = n_grp * rows
    barrier = pltpu.get_barrier_semaphore()
    for k in range(1, n_grp):
        pl.semaphore_signal(barrier, inc=1, device_id={"grp": lax.rem(g + k, n_grp)})
    for k in range(1, n_dom):
        pl.semaphore_signal(barrier, inc=1, device_id={"dom": lax.rem(me + k, n_dom)})
    pl.semaphore_wait(barrier, n_grp + n_dom - 2)

    def line_copy(direction, step, r, src, origin):
        target = g + 1 if direction == 0 else g - 1
        return pltpu.make_async_remote_copy(
            src_ref=src,
            dst_ref=table.at[origin * rows + r],
            send_sem=line_send.at[direction, step, r],
            recv_sem=line_recv.at[direction, step, r],
            device_id={"grp": target},
        )

    can_send = (g < n_grp - 1, g > 0)
    for r in range(rows):
        for direction in range(2):
            @pl.when(can_send[direction])
            def _():
                line_copy(direction, 0, r, panels.at[r], g).start()

    def meta_copy(k, over_dom):
        if over_dom:
            target = lax.rem(me + k, n_dom)
            return pltpu.make_async_remote_copy(
                src_ref=dom_meta.at[target], dst_ref=meta.at[n_grp + me],
                send_sem=meta_send.at[n_grp + k], recv_sem=meta_recv.at[n_grp + k],
                device_id={"dom": target},
            )
        return pltpu.make_async_remote_copy(
            src_ref=grp_meta, dst_ref=meta.at[g],
            send_sem=meta_send.at[k], recv_sem=meta_recv.at[k],
            device_id={"grp": lax.rem(g + k, n_grp)},
        )

    def dom_copy(k):
        target = lax.rem(me + k, n_dom)
        return pltpu.make_async_remote_copy(
            src_ref=outgoing.at[pl.ds(target * hs, hs)],
            dst_ref=table.at[pl.ds(far_base + me * hs, hs)],
            send_sem=dom_send.at[k], recv_sem=dom_recv.at[k],
            device_id={"dom": target},
        )

    for k in range(1, n_grp):
        meta_copy(k, False).start()
    for k in range(1, n_dom):
        dom_copy(k).start()
        meta_copy(k, True).start()
    own = (
        pltpu.make_async_copy(panels, table.at[pl.ds(g * rows, rows)], own_sem.at[0]),
        pltpu.make_async_copy(outgoing.at[pl.ds(me * hs, hs)], table.at[pl.ds(far_base + me * hs, hs)], own_sem.at[1]),
        pltpu.make_async_copy(grp_meta, meta.at[g], own_sem.at[2]),
        pltpu.make_async_copy(dom_meta.at[me], meta.at[n_grp + me], own_sem.at[3]),
    )
    for copy in own:
        copy.start()

    def origin_of(direction, step):
        return g - 1 - step if direction == 0 else g + 1 + step

    for step in range(n_grp - 1):
        for r in range(rows):
            for direction in range(2):
                origin = origin_of(direction, step)
                exists = (origin >= 0) & (origin < n_grp)

                @pl.when(exists)
                def _():
                    src = table.at[origin * rows + r]
                    line_copy(direction, step, r, src, origin).wait_recv()

                if step < n_grp - 2:
                    @pl.when(exists & can_send[direction])
                    def _():
                        src = table.at[origin * rows + r]
                        line_copy(direction, step + 1, r, src, origin).start()

    for copy in own:
        copy.wait()
    for k in range(1, n_grp):
        meta_copy(k, False).wait()
    for k in range(1, n_dom):
        dom_copy(k).wait()
        meta_copy(k, True).wait()
    for step in range(n_grp - 1):
        for r in range(rows):
            for direction in range(2):
                origin = g - step if direction == 0 else g + step
                exists = (origin >= 0) & (origin < n_grp)

                @pl.when(exists & can_send[direction])
                def _():
                    line_copy(direction, step, r, panels.at[r], origin).wait_send()


def split_pair(x):
    high = x.astype(jnp.bfloat16)
    low = (x - high.astype(jnp.float32)).astype(jnp.bfloat16)
    return high, low


def product_kernel(
    n_grp, n_dom, rows, hs, ka, kp, kc, cap,
    cols, halo, slots, owner, meta,
    operator, table, prolong,
    out,
    split_table, total,
):
    k = pl.program_id(0)
    me = lax.axis_index("dom")
    panel_count = table.shape[0]
    near_count = n_grp * rows
    lane = lax.broadcasted_iota(jnp.int32, (BS, LANES), 1) < BS

    @pl.when(k == 0)
    def _():
        def clear(e, carry):
            total[e] = jnp.zeros(total.shape[1:], jnp.float32)
            return carry

        lax.fori_loop(0, total.shape[0], clear, 0)

        def split(p, carry):
            high, low = split_pair(table[p])
            split_table[p, 0:BS] = high
            split_table[p, BS:2 * BS] = low
            split_table[p, 2 * BS:3 * BS] = high
            return carry

        lax.fori_loop(0, panel_count, split, 0)

        def pair(step, carry):
            i = step // ka
            m = step % ka
            col = cols[i, m]
            near = m < KG

            @pl.when(near | (m - KG < halo[i]))
            def _():
                panel = jnp.where(near, col, near_count + col)
                meta_row = jnp.where(near, col // rows, n_grp + col // hs)
                meta_lane = jnp.where(near, (col % rows) * kp, (col % hs) * kp)
                high, low = split_pair(operator[i, m])
                high = high.astype(jnp.float32)
                low = low.astype(jnp.float32)
                left = jnp.concatenate([high, high, low], axis=1).astype(jnp.bfloat16)
                w = jnp.dot(left, split_table[panel], preferred_element_type=jnp.float32)
                for q in range(0, kp, 2):
                    piece = w[:, q * BS:(q + 2) * BS]
                    first = meta[meta_row, meta_lane + q]
                    second = meta[meta_row, meta_lane + q + 1]
                    total[first, i] += jnp.where(lane, piece, 0.0)
                    total[second, i] += jnp.where(lane, 0.0, piece)

            return carry

        lax.fori_loop(0, rows * ka, pair, 0)

    own_extra = k >= n_dom
    owner_dom = jnp.where(own_extra, me, k)
    slot = jnp.where(own_extra, me * cap + 1 + k - n_dom, k * cap)
    owner_row = owner[slot]
    pattern_at = hs * kp + owner_row * kc
    left = []
    for i in range(rows):
        place = jnp.int32(kp)
        for j in range(kp):
            place = jnp.where(slots[i, j] == slot, j, place)
        block = prolong[i, jnp.minimum(place, kp - 1)]
        left.append(jnp.where(place < kp, block, 0.0).T)
    left = jnp.concatenate(left, axis=1)
    left_high, left_low = split_pair(left)
    both = jnp.concatenate([left_high, left_low], axis=0)
    wide = lax.broadcasted_iota(jnp.int32, (rows, BS, LANES), 2) < BS
    for c in range(0, kc, 4):
        highs = []
        lows = []
        for h in range(2):
            first = total[meta[n_grp + owner_dom, pattern_at + c + 2 * h]]
            second = total[meta[n_grp + owner_dom, pattern_at + c + 2 * h + 1]]
            kept = jnp.where(wide, first, second).reshape(rows * BS, LANES)
            turned = pltpu.roll(jnp.where(wide, second, first).reshape(rows * BS, LANES), BS, 1)
            high, low = split_pair(kept + turned)
            highs.append(high)
            lows.append(low)
        high = jnp.concatenate(highs, axis=1)
        low = jnp.concatenate(lows, axis=1)
        stacked = jnp.dot(both, high, preferred_element_type=jnp.float32)
        rest = jnp.dot(left_high, low, preferred_element_type=jnp.float32)
        out[0, :, c * BS:(c + 4) * BS] = stacked[:BS] + stacked[BS:] + rest


def reduce_kernel(
    n_grp, n_dom, cap, row_at,
    owner, meta, partial,
    out,
    arrived, send_sem, recv_sem,
):
    me = lax.axis_index("dom")
    barrier = pltpu.get_barrier_semaphore()
    for k in range(1, n_dom):
        pl.semaphore_signal(barrier, inc=1, device_id={"dom": lax.rem(me + k, n_dom)})
    pl.semaphore_wait(barrier, n_dom - 1)

    def copy_of(k):
        target = lax.rem(me + k, n_dom)
        return pltpu.make_async_remote_copy(
            src_ref=partial.at[target], dst_ref=arrived.at[k - 1],
            send_sem=send_sem.at[k - 1], recv_sem=recv_sem.at[k - 1],
            device_id={"dom": target},
        )

    for k in range(1, n_dom):
        copy_of(k).start()
    owned = out.shape[0]
    for r in range(owned):
        value = partial[me] * (owner[me * cap] == r).astype(jnp.float32)
        for t in range(1, cap):
            value += partial[n_dom + t - 1] * (owner[me * cap + t] == r).astype(jnp.float32)
        out[r] = value
    for k in range(1, n_dom):
        copy_of(k).wait_recv()
        source = lax.rem(me - k + n_dom, n_dom)
        row = meta[n_grp + source, row_at]
        for r in range(owned):
            out[r] += arrived[k - 1] * (row == r).astype(jnp.float32)
    for k in range(1, n_dom):
        copy_of(k).wait_send()


def per_device(
    operator_blocks, operator_cols, halo_count, prolong_blocks, prolong_cols,
    prolong_slot, send_lists, slot_owner_row, coarse_pattern,
):
    n_grp = lax.axis_size("grp")
    n_dom = lax.axis_size("dom")
    rows, ka = operator_cols.shape
    kp = prolong_cols.shape[1]
    owned, kc = coarse_pattern.shape
    hs = send_lists.shape[1] // n_dom
    cap = slot_owner_row.shape[1] // n_dom
    owner = slot_owner_row.reshape(n_dom * cap)
    total_ids = owned * n_grp * n_dom
    used = n_dom + cap - 1
    panel_count = n_grp * rows + n_dom * hs

    prolong = prolong_blocks.reshape(rows, kp, BS, BS)
    panels = prolong.transpose(0, 2, 1, 3).reshape(rows, BS, kp * BS)
    picked = send_lists.reshape(n_dom * hs)
    outgoing = jnp.take(panels, picked, axis=0, mode="clip")
    grp_meta = jnp.pad(prolong_cols.reshape(1, rows * kp), ((0, 0), (0, LANES - rows * kp)))
    row_at = hs * kp + owned * kc
    dom_meta = jnp.concatenate(
        [
            jnp.take(prolong_cols, picked, axis=0, mode="clip").reshape(n_dom, hs * kp),
            jnp.broadcast_to(coarse_pattern.reshape(1, owned * kc), (n_dom, owned * kc)),
            owner.reshape(n_dom, cap)[:, :1],
            jnp.zeros((n_dom, LANES - row_at - 1), jnp.int32),
        ],
        axis=1,
    ).reshape(n_dom, 1, LANES)

    sem = pltpu.SemaphoreType.DMA
    table, meta = pl.pallas_call(
        functools.partial(gather_kernel, n_grp, n_dom, rows, hs),
        out_shape=(
            jax.ShapeDtypeStruct((panel_count, BS, kp * BS), jnp.float32),
            jax.ShapeDtypeStruct((n_grp + n_dom, 1, LANES), jnp.int32),
        ),
        in_specs=[vmem_spec()] * 4,
        out_specs=(any_spec(), any_spec()),
        scratch_shapes=[
            sem((4,)), sem((2, n_grp - 1, rows)), sem((2, n_grp - 1, rows)),
            sem((n_dom,)), sem((n_dom,)), sem((n_grp + n_dom,)), sem((n_grp + n_dom,)),
        ],
        compiler_params=pltpu.CompilerParams(collective_id=0, has_side_effects=True),
        name="gather_rows",
    )(panels, outgoing, dom_meta, grp_meta)
    meta = meta.reshape(n_grp + n_dom, LANES)

    whole = lambda shape: pl.BlockSpec(shape, lambda k: (0,) * len(shape), pipeline_mode=pl.Buffered(1))
    partial = pl.pallas_call(
        functools.partial(product_kernel, n_grp, n_dom, rows, hs, ka, kp, kc, cap),
        grid=(used,),
        out_shape=jax.ShapeDtypeStruct((used, BS, kc * BS), jnp.float32),
        in_specs=[smem_spec()] * 5 + [
            whole((rows, ka, BS, BS)), whole((panel_count, BS, kp * BS)), whole((rows, kp, BS, BS)),
        ],
        out_specs=pl.BlockSpec((1, BS, kc * BS), lambda k: (k, 0, 0)),
        scratch_shapes=[
            pltpu.VMEM((panel_count, 3 * BS, kp * BS), jnp.bfloat16),
            pltpu.VMEM((total_ids, rows, BS, LANES), jnp.float32),
        ],
        compiler_params=pltpu.CompilerParams(vmem_limit_bytes=63000 * 1024),
        name="block_products",
    )(
        operator_cols, halo_count, prolong_slot, owner, meta,
        operator_blocks.reshape(rows, ka, BS, BS), table, prolong,
    )

    summed = pl.pallas_call(
        functools.partial(reduce_kernel, n_grp, n_dom, cap, row_at),
        out_shape=jax.ShapeDtypeStruct((owned, BS, kc * BS), jnp.float32),
        in_specs=[smem_spec(), smem_spec(), vmem_spec()],
        out_specs=vmem_spec(),
        scratch_shapes=[
            pltpu.VMEM((n_dom - 1, BS, kc * BS), jnp.float32),
            sem((n_dom - 1,)), sem((n_dom - 1,)),
        ],
        compiler_params=pltpu.CompilerParams(collective_id=1, has_side_effects=True),
        name="sum_rows",
    )(owner, meta, partial)
    return summed.reshape(owned, BS, kc, BS).transpose(0, 2, 1, 3).reshape(owned, kc, BS * BS)


def solution(mesh):
    blocks = P(("grp", "dom"), None, None)
    lists = P(("grp", "dom"), None)
    return jax.shard_map(
        per_device,
        mesh=mesh,
        in_specs=(blocks, lists, P(("grp", "dom")), blocks, lists, lists, lists, lists, lists),
        out_specs=blocks,
        check_vma=False,
    )
```

profile of v0, /device:TPU:0, one launch (start us, length us, event | category | flops | bytes accessed | tf_op | source)
XLA Modules:
  0.0 112.6 jit_solution(6315004758117741213)
XLA Ops:
  0.0 0.5 broadcast.15
  0.5 1.3 %reduce.3 = s32[16]{0:T(128)S(1)} reduce(s32[1,16]{1,0:T(1,128)} %param.16, s32[]{:T(128)} %broadcast.15), dimensions={0}, to_apply=%param.16.reduce_sub_computation.3 | reduce | bytes 132 | tf_op args[7]
  1.8 0.8 reshape.64
  2.6 0.1 pad.6.clone
  2.7 0.8 reshape.35
  3.4 0.5 pad.4.grp_meta
  3.9 0.1 pad.8.clone
  4.0 0.1 reshape_reshape.3
  4.1 0.7 pad_clamp_fusion
  4.8 1.2 %gather_fusion.1 = s32[8,8]{1,0:T(8,128)S(1)} fusion(s32[4,8]{1,0:T(4,128)} %param.13, s32[1024]{0:T(1024)S(1)} %pad_clamp_fusion), kind=kCustom, calls=%fused_computation.1 | custom fusion | bytes 544 | tf_op jit(solution)/shard_map/jit(_take)/gather | solution.py:295
  6.0 0.7 add_add_fusion
  6.7 1.5 %reshape.32.prolong = f32[4,8,64,64]{3,2,1,0:T(8,128)S(1)} reshape(f32[4,8,4096]{2,1,0:T(8,128)} %param.12) | data formatting | bytes 1048576 | tf_op jit(solution)/shard_map/reshape | solution.py:287
  8.1 0.0 copy-start
  8.1 0.6 copy.11
  8.8 0.3 reshape.33.panels
  9.0 0.0 copy-start.1
  9.1 0.0 copy-start.2
  9.1 1.6 %gather_fusion = f32[8,64,512]{2,1,0:T(8,128)} fusion(f32[4,64,512]{2,1,0:T(8,128)S(1)} %reshape.33.panels, s32[1024]{0:T(1024)S(1)} %pad_clamp_fusion), kind=kCustom, calls=%fused_computation | custom fusion | bytes 2097184 | tf_op jit(solution)/shard_map/jit(_take)/gather | solution.py:290
  10.7 0.0 copy-done
  10.7 0.0 copy-done.1
  10.7 42.6 %gather_rows.1 = (f32[24,64,512]{2,1,0:T(8,128)}, s32[12,1,128]{2,1,0:T(1,128)}) custom-call(f32[4,64,512]{2,1,0:T(8,128)} %copy-done.1, f32[8,64,512]{2,1,0:T(8,128)} %gather_fusion, s32[8,1,128]{2,1,0:T(1,128)} %bitcast.17, s32[1,128]{1,0:T(1,128)} %pad.4.grp_meta), custom_call_target="tpu_custom_call" | custom-call | tf_op jit(solution)/shard_map/gather_rows/pallas_call | solution.py:304
  53.2 1.3 %copy.15 = s32[12,1,128]{2,0,1:T(8,128)} copy(s32[12,1,128]{2,1,0:T(1,128)} %get-tuple-element.7) | data formatting | bytes 12288
  54.5 0.0 copy-done.2
  54.5 2.2 %reshape.37.operator = f32[4,16,64,64]{3,2,1,0:T(8,128)} reshape(f32[4,16,4096]{2,1,0:T(8,128)S(1)} %copy-done.2) | data formatting | bytes 2097152 | tf_op jit(solution)/shard_map/reshape | solution.py:338
  56.7 25.9 %block_products.1.partial = f32[9,64,1024]{2,1,0:T(8,128)} custom-call(s32[4,16]{1,0:T(4,128)} %cols.1, s32[4]{0:T(128)} %halo.1, s32[4,8]{1,0:T(4,128)} %slots.1, s32[16]{0:T(128)} %bitcast.19, s32[12,128]{1,0:T(8,128)} %bitcast.15, f32[4,16,64,64]{3,2,1,0:T(8,128)} %reshape.37.operator, f32[24,64,512]{2,1,0:T(8,128)} %get-tuple-element.8.table, ...), custom_call_target="tpu_custom_call" | custom-call | tf_op jit(solution)/shard_map/block_products/pallas_call | solution.py:322
  82.6 27.2 %sum_rows.1 = f32[2,64,1024]{2,1,0:T(8,128)} custom-call(s32[16]{0:T(128)} %bitcast.20, s32[12,128]{1,0:T(8,128)} %bitcast.16, f32[9,64,1024]{2,1,0:T(8,128)} %block_products.1.partial), custom_call_target="tpu_custom_call" | custom-call | tf_op jit(solution)/shard_map/sum_rows/pallas_call | solution.py:341
  109.8 1.3 %reshape.38 = f32[2,64,16,64]{3,2,1,0:T(8,128)S(1)} reshape(f32[2,64,1024]{2,1,0:T(8,128)} %sum_rows.1) | data formatting | bytes 1048576 | tf_op jit(solution)/shard_map/reshape | solution.py:353
  111.1 0.3 copy.12
  111.4 1.2 %reshape.39 = f32[2,16,4096]{2,1,0:T(8,128)} reshape(f32[2,16,64,64]{3,2,1,0:T(8,128)S(1)} %copy.12) | data formatting | bytes 1048576 | tf_op jit(solution)/shard_map/reshape | solution.py:353
  (1 shorter events, 0.0 us)
Async XLA Ops:
  8.1 2.5 %copy-start = (f32[4,8,64,64]{3,2,1,0:T(8,128)}, f32[4,8,64,64]{3,2,1,0:T(8,128)S(1)}, u32[]{:S(2)}) copy-start(f32[4,8,64,64]{3,2,1,0:T(8,128)S(1)} %reshape.32.prolong) | copy-start | bytes 1572868
  9.0 1.6 %copy-start.1 = (f32[4,64,512]{2,1,0:T(8,128)}, f32[4,64,512]{2,1,0:T(8,128)S(1)}, u32[]{:S(2)}) copy-start(f32[4,64,512]{2,1,0:T(8,128)S(1)} %reshape.33.panels) | copy-start | bytes 1572868
  9.1 45.5 %copy-start.2 = (f32[4,16,4096]{2,1,0:T(8,128)S(1)}, f32[4,16,4096]{2,1,0:T(8,128)}, u32[]{:S(2)}) copy-start(f32[4,16,4096]{2,1,0:T(8,128)} %param.9) | copy-start | bytes 3145732
where the time goes:
time: 114 us; the launch traced here: 113 us
  Pallas kernels  95.6 us (84%)
  local copies, waits for them, and re-layouts  14.2 us (12%)
  other arithmetic  2.65 us (2%)
    pallas_call x1, Pallas kernels, per_device(): pl.pallas_call(functools.partial(gather_kernel, n_grp, n_dom, rows, hs),...  42.6 us
    pallas_call x1, Pallas kernels, per_device(): pl.pallas_call(functools.partial(reduce_kernel, n_grp, n_dom, cap, row_at...  27.2 us
    pallas_call x1, Pallas kernels, per_device(): pl.pallas_call(functools.partial(product_kernel, n_grp, n_dom, rows, hs,...  25.9 us
    reshape x2, local copies, waits for them, and re-layouts, per_device(): summed.reshape(owned, BS, kc, BS).transpose(0, 2, 1, 3)  2.46 us

commit v1 on v0

--- a/solution.py
+++ b/solution.py
@@ -27,8 +27,8 @@
 
 def gather_kernel(
     n_grp, n_dom, rows, hs,
-    panels, outgoing, dom_meta, grp_meta,
-    table, meta,
+    panels, outgoing, dom_meta, grp_meta, operator,
+    table, meta, blocks,
     own_sem, line_send, line_recv, dom_send, dom_recv, meta_send, meta_recv,
 ):
     g = lax.axis_index("grp")
@@ -95,6 +95,14 @@
     for copy in own:
         copy.start()
 
+    def relay_row(i, carry):
+        row = operator[i]
+        for a in range(BS):
+            blocks[i, :, a, :] = row[:, a * BS:(a + 1) * BS]
+        return carry
+
+    lax.fori_loop(0, rows, relay_row, 0)
+
     def origin_of(direction, step):
         return g - 1 - step if direction == 0 else g + 1 + step
 
@@ -140,14 +148,13 @@
 
 
 def product_kernel(
-    n_grp, n_dom, rows, hs, ka, kp, kc, cap,
-    cols, halo, slots, owner, meta,
-    operator, table, prolong,
+    n_grp, n_dom, rows, hs, ka, kp,
+    cols, halo, meta,
+    operator, table,
     out,
     split_table, total,
 ):
     k = pl.program_id(0)
-    me = lax.axis_index("dom")
     panel_count = table.shape[0]
     near_count = n_grp * rows
     lane = lax.broadcasted_iota(jnp.int32, (BS, LANES), 1) < BS
@@ -196,68 +203,84 @@
 
         lax.fori_loop(0, rows * ka, pair, 0)
 
-    own_extra = k >= n_dom
-    owner_dom = jnp.where(own_extra, me, k)
-    slot = jnp.where(own_extra, me * cap + 1 + k - n_dom, k * cap)
-    owner_row = owner[slot]
-    pattern_at = hs * kp + owner_row * kc
-    left = []
-    for i in range(rows):
-        place = jnp.int32(kp)
-        for j in range(kp):
-            place = jnp.where(slots[i, j] == slot, j, place)
-        block = prolong[i, jnp.minimum(place, kp - 1)]
-        left.append(jnp.where(place < kp, block, 0.0).T)
-    left = jnp.concatenate(left, axis=1)
-    left_high, left_low = split_pair(left)
-    both = jnp.concatenate([left_high, left_low], axis=0)
-    wide = lax.broadcasted_iota(jnp.int32, (rows, BS, LANES), 2) < BS
-    for c in range(0, kc, 4):
-        highs = []
-        lows = []
-        for h in range(2):
-            first = total[meta[n_grp + owner_dom, pattern_at + c + 2 * h]]
-            second = total[meta[n_grp + owner_dom, pattern_at + c + 2 * h + 1]]
-            kept = jnp.where(wide, first, second).reshape(rows * BS, LANES)
-            turned = pltpu.roll(jnp.where(wide, second, first).reshape(rows * BS, LANES), BS, 1)
-            high, low = split_pair(kept + turned)
-            highs.append(high)
-            lows.append(low)
-        high = jnp.concatenate(highs, axis=1)
-        low = jnp.concatenate(lows, axis=1)
-        stacked = jnp.dot(both, high, preferred_element_type=jnp.float32)
-        rest = jnp.dot(left_high, low, preferred_element_type=jnp.float32)
-        out[0, :, c * BS:(c + 4) * BS] = stacked[:BS] + stacked[BS:] + rest
-
-
-def reduce_kernel(
-    n_grp, n_dom, cap, row_at,
-    owner, meta, partial,
+    chunk = out.shape[0]
+    half = lax.broadcasted_iota(jnp.int32, (rows * BS, LANES), 1) < BS
+
+    def fold(t, carry):
+        value = total[k * chunk + t].reshape(rows * BS, LANES)
+        value += pltpu.roll(value, BS, 1)
+        high = value.astype(jnp.bfloat16).astype(jnp.float32)
+        out[t] = jnp.where(half, high, value - high).astype(jnp.bfloat16)
+        return carry
+
+    lax.fori_loop(0, chunk, fold, 0)
+
+
+def exchange_kernel(
+    n_grp, n_dom, rows, hs, kp, kc, cap, row_at,
+    slots, owner, meta, packed, prolong,
     out,
-    arrived, send_sem, recv_sem,
+    partial, arrived, send_sem, recv_sem,
 ):
     me = lax.axis_index("dom")
     barrier = pltpu.get_barrier_semaphore()
     for k in range(1, n_dom):
         pl.semaphore_signal(barrier, inc=1, device_id={"dom": lax.rem(me + k, n_dom)})
     pl.semaphore_wait(barrier, n_dom - 1)
+    lane = lax.broadcasted_iota(jnp.int32, (BS, LANES), 1) < BS
+
+    def slot_rows(owner_dom, slot, at):
+        owner_row = owner[0, slot]
+        pattern_at = hs * kp + owner_row * kc
+        left = []
+        for i in range(rows):
+            place = jnp.int32(kp)
+            for j in range(kp):
+                place = jnp.where(slots[i, j] == slot, j, place)
+            block = prolong[i, jnp.minimum(place, kp - 1)]
+            left.append(jnp.where(place < kp, block, 0.0).T)
+        left_high, left_low = split_pair(jnp.concatenate(left, axis=1))
+        both = jnp.concatenate([left_high, left_low], axis=0)
+        for c in range(0, kc, 2):
+            right = jnp.concatenate(
+                [packed[meta[n_grp + owner_dom, pattern_at + c + h]] for h in range(2)], axis=1
+            )
+            stacked = jnp.dot(both, right, preferred_element_type=jnp.float32)
+            both_sum = stacked[:BS] + stacked[BS:]
+            folded = []
+            for h in range(2):
+                piece = both_sum[:, h * LANES:(h + 1) * LANES]
+                folded.append(piece + pltpu.roll(piece, BS, 1))
+            partial[at, :, c * BS:(c + 2) * BS] = jnp.where(lane, folded[0], folded[1])
 
     def copy_of(k):
         target = lax.rem(me + k, n_dom)
         return pltpu.make_async_remote_copy(
-            src_ref=partial.at[target], dst_ref=arrived.at[k - 1],
+            src_ref=partial.at[k], dst_ref=arrived.at[k - 1],
             send_sem=send_sem.at[k - 1], recv_sem=recv_sem.at[k - 1],
             device_id={"dom": target},
         )
 
-    for k in range(1, n_dom):
-        copy_of(k).start()
+    def far_slot(k, carry):
+        target = lax.rem(me + k, n_dom)
+        slot_rows(target, target * cap, k)
+
+        @pl.when(k > 1)
+        def _():
+            copy_of(k - 1).start()
+
+        return carry
+
+    lax.fori_loop(1, n_dom, far_slot, 0)
+    slot_rows(me, me * cap, 0)
+    copy_of(n_dom - 1).start()
     owned = out.shape[0]
     for r in range(owned):
-        value = partial[me] * (owner[me * cap] == r).astype(jnp.float32)
-        for t in range(1, cap):
-            value += partial[n_dom + t - 1] * (owner[me * cap + t] == r).astype(jnp.float32)
-        out[r] = value
+        out[r] = partial[0] * (owner[0, me * cap] == r).astype(jnp.float32)
+    for t in range(1, cap):
+        slot_rows(me, me * cap + t, n_dom + t - 1)
+        for r in range(owned):
+            out[r] += partial[n_dom + t - 1] * (owner[0, me * cap + t] == r).astype(jnp.float32)
     for k in range(1, n_dom):
         copy_of(k).wait_recv()
         source = lax.rem(me - k + n_dom, n_dom)
@@ -266,6 +289,38 @@
             out[r] += arrived[k - 1] * (row == r).astype(jnp.float32)
     for k in range(1, n_dom):
         copy_of(k).wait_send()
+
+
+def prepare_kernel(
+    n_dom, rows, hs, kp, kc, cap,
+    picked, owner, prolong_raw, prolong_cols, pattern,
+    panels, outgoing, prolong, dom_meta, grp_meta,
+):
+    owned = pattern.shape[0]
+    for i in range(rows):
+        raw = prolong_raw[i]
+        for a in range(BS):
+            prolong[i, :, a, :] = raw[:, a * BS:(a + 1) * BS]
+        for q in range(0, kp, 2):
+            panels[i, :, q * BS:(q + 2) * BS] = jnp.concatenate([prolong[i, q], prolong[i, q + 1]], axis=1)
+    grp_meta[...] = jnp.zeros(grp_meta.shape, jnp.int32)
+    dom_meta[...] = jnp.zeros(dom_meta.shape, jnp.int32)
+    for i in range(rows):
+        grp_meta[:, i * kp:(i + 1) * kp] = prolong_cols[i:i + 1, :]
+    row_at = hs * kp + owned * kc
+
+    def for_dom(d, carry):
+        for h in range(hs):
+            row = picked[0, d * hs + h]
+            outgoing[d * hs + h] = panels[row]
+            dom_meta[d, :, h * kp:(h + 1) * kp] = prolong_cols[pl.ds(row, 1), :]
+        for r in range(owned):
+            at = hs * kp + r * kc
+            dom_meta[d, :, at:at + kc] = pattern[r:r + 1, :]
+        dom_meta[d, :, row_at:row_at + 1] = jnp.full((1, 1), owner[0, d * cap], jnp.int32)
+        return carry
+
+    lax.fori_loop(0, n_dom, for_dom, 0)
 
 
 def per_device(
@@ -279,77 +334,72 @@
     owned, kc = coarse_pattern.shape
     hs = send_lists.shape[1] // n_dom
     cap = slot_owner_row.shape[1] // n_dom
-    owner = slot_owner_row.reshape(n_dom * cap)
     total_ids = owned * n_grp * n_dom
     used = n_dom + cap - 1
     panel_count = n_grp * rows + n_dom * hs
-
-    prolong = prolong_blocks.reshape(rows, kp, BS, BS)
-    panels = prolong.transpose(0, 2, 1, 3).reshape(rows, BS, kp * BS)
-    picked = send_lists.reshape(n_dom * hs)
-    outgoing = jnp.take(panels, picked, axis=0, mode="clip")
-    grp_meta = jnp.pad(prolong_cols.reshape(1, rows * kp), ((0, 0), (0, LANES - rows * kp)))
     row_at = hs * kp + owned * kc
-    dom_meta = jnp.concatenate(
-        [
-            jnp.take(prolong_cols, picked, axis=0, mode="clip").reshape(n_dom, hs * kp),
-            jnp.broadcast_to(coarse_pattern.reshape(1, owned * kc), (n_dom, owned * kc)),
-            owner.reshape(n_dom, cap)[:, :1],
-            jnp.zeros((n_dom, LANES - row_at - 1), jnp.int32),
-        ],
-        axis=1,
-    ).reshape(n_dom, 1, LANES)
+    f32 = lambda *shape: jax.ShapeDtypeStruct(shape, jnp.float32)
+    i32 = lambda *shape: jax.ShapeDtypeStruct(shape, jnp.int32)
+
+    panels, outgoing, prolong, dom_meta, grp_meta = pl.pallas_call(
+        functools.partial(prepare_kernel, n_dom, rows, hs, kp, kc, cap),
+        out_shape=(
+            f32(rows, BS, kp * BS), f32(n_dom * hs, BS, kp * BS), f32(rows, kp, BS, BS),
+            i32(n_dom, 1, LANES), i32(1, LANES),
+        ),
+        in_specs=[smem_spec()] * 2 + [vmem_spec()] * 3,
+        out_specs=(vmem_spec(),) * 5,
+        name="prepare",
+    )(send_lists, slot_owner_row, prolong_blocks, prolong_cols, coarse_pattern)
 
     sem = pltpu.SemaphoreType.DMA
-    table, meta = pl.pallas_call(
+    table, meta, blocks = pl.pallas_call(
         functools.partial(gather_kernel, n_grp, n_dom, rows, hs),
         out_shape=(
-            jax.ShapeDtypeStruct((panel_count, BS, kp * BS), jnp.float32),
-            jax.ShapeDtypeStruct((n_grp + n_dom, 1, LANES), jnp.int32),
+            f32(panel_count, BS, kp * BS), i32(n_grp + n_dom, 1, LANES), f32(rows, ka, BS, BS),
         ),
-        in_specs=[vmem_spec()] * 4,
-        out_specs=(any_spec(), any_spec()),
+        in_specs=[vmem_spec()] * 5,
+        out_specs=(any_spec(), any_spec(), vmem_spec()),
         scratch_shapes=[
             sem((4,)), sem((2, n_grp - 1, rows)), sem((2, n_grp - 1, rows)),
             sem((n_dom,)), sem((n_dom,)), sem((n_grp + n_dom,)), sem((n_grp + n_dom,)),
         ],
         compiler_params=pltpu.CompilerParams(collective_id=0, has_side_effects=True),
         name="gather_rows",
-    )(panels, outgoing, dom_meta, grp_meta)
+    )(panels, outgoing, dom_meta, grp_meta, operator_blocks)
     meta = meta.reshape(n_grp + n_dom, LANES)
 
     whole = lambda shape: pl.BlockSpec(shape, lambda k: (0,) * len(shape), pipeline_mode=pl.Buffered(1))
-    partial = pl.pallas_call(
-        functools.partial(product_kernel, n_grp, n_dom, rows, hs, ka, kp, kc, cap),
-        grid=(used,),
-        out_shape=jax.ShapeDtypeStruct((used, BS, kc * BS), jnp.float32),
-        in_specs=[smem_spec()] * 5 + [
-            whole((rows, ka, BS, BS)), whole((panel_count, BS, kp * BS)), whole((rows, kp, BS, BS)),
-        ],
-        out_specs=pl.BlockSpec((1, BS, kc * BS), lambda k: (k, 0, 0)),
+    chunk = 8
+    packed = pl.pallas_call(
+        functools.partial(product_kernel, n_grp, n_dom, rows, hs, ka, kp),
+        grid=(total_ids // chunk,),
+        out_shape=jax.ShapeDtypeStruct((total_ids, rows * BS, LANES), jnp.bfloat16),
+        in_specs=[smem_spec()] * 3 + [whole((rows, ka, BS, BS)), whole((panel_count, BS, kp * BS))],
+        out_specs=pl.BlockSpec((chunk, rows * BS, LANES), lambda k: (k, 0, 0)),
         scratch_shapes=[
             pltpu.VMEM((panel_count, 3 * BS, kp * BS), jnp.bfloat16),
             pltpu.VMEM((total_ids, rows, BS, LANES), jnp.float32),
         ],
         compiler_params=pltpu.CompilerParams(vmem_limit_bytes=63000 * 1024),
         name="block_products",
-    )(
-        operator_cols, halo_count, prolong_slot, owner, meta,
-        operator_blocks.reshape(rows, ka, BS, BS), table, prolong,
-    )
+    )(operator_cols, halo_count, meta, blocks, table)
 
     summed = pl.pallas_call(
-        functools.partial(reduce_kernel, n_grp, n_dom, cap, row_at),
-        out_shape=jax.ShapeDtypeStruct((owned, BS, kc * BS), jnp.float32),
-        in_specs=[smem_spec(), smem_spec(), vmem_spec()],
+        functools.partial(exchange_kernel, n_grp, n_dom, rows, hs, kp, kc, cap, row_at),
+        out_shape=f32(owned, BS, kc * BS),
+        in_specs=[smem_spec()] * 3 + [vmem_spec()] * 2,
         out_specs=vmem_spec(),
         scratch_shapes=[
+            pltpu.VMEM((used, BS, kc * BS), jnp.float32),
             pltpu.VMEM((n_dom - 1, BS, kc * BS), jnp.float32),
             sem((n_dom - 1,)), sem((n_dom - 1,)),
         ],
-        compiler_params=pltpu.CompilerParams(collective_id=1, has_side_effects=True),
+        compiler_params=pltpu.CompilerParams(
+            collective_id=1, has_side_effects=True, vmem_limit_bytes=63000 * 1024
+        ),
         name="sum_rows",
-    )(owner, meta, partial)
+    )(prolong_slot, slot_owner_row, meta, packed, prolong)
     return summed.reshape(owned, BS, kc, BS).transpose(0, 2, 1, 3).reshape(owned, kc, BS * BS)
 
 

time: 114 us -> 110 us (0.965)
  local copies, waits for them, and re-layouts: 14.2 us -> 4.07 us
  Pallas kernels: 95.6 us -> 105 us
  other arithmetic: 2.65 us -> 0 us
    pallas_call x1 -> x2, Pallas kernels: 27.2 us -> 34.4 us  [the longest x1 29.8 us: per_device(): pl.pallas_call(functools.partial(exchange_kernel, n_grp, n_dom, rows, hs,...]
    reshape x4 -> x0, local copies, waits for them, and re-layouts: 4.68 us -> none  [the longest x1 2.2 us: per_device(): operator_blocks.reshape(rows, ka, BS, BS)]
    gather x2 -> x0, local copies, waits for them, and re-layouts: 2.83 us -> none  [the longest x1 1.59 us: per_device(): outgoing = jnp.take(panels, picked, axis=0, mode='clip')]
    pallas_call x1, Pallas kernels: 42.6 us -> 44.3 us  [per_device(): pl.pallas_call(functools.partial(gather_kernel, n_grp, n_dom, rows, hs),...]
    unnamed x1 -> x0, other arithmetic: 1.32 us -> none
where the time goes in v1:
time: 110 us
  Pallas kernels  105 us (95%)
  local copies, waits for them, and re-layouts  4.07 us (4%)
    pallas_call x1, Pallas kernels, per_device(): pl.pallas_call(functools.partial(gather_kernel, n_grp, n_dom, rows, hs),...  44.3 us
    pallas_call x1, Pallas kernels, per_device(): pl.pallas_call(functools.partial(exchange_kernel, n_grp, n_dom, rows, hs,...  29.8 us
    pallas_call x1, Pallas kernels, per_device(): pl.pallas_call(functools.partial(product_kernel, n_grp, n_dom, rows, hs,...  26.7 us
    pallas_call x1, Pallas kernels, per_device(): pl.pallas_call(functools.partial(prepare_kernel, n_dom, rows, hs, kp, kc,...  4.59 us
    reshape x2, local copies, waits for them, and re-layouts, per_device(): summed.reshape(owned, BS, kc, BS).transpose(0, 2, 1, 3)  2.46 us

profile of v1, /device:TPU:0, one launch (start us, length us, event | category | flops | bytes accessed | tf_op | source)
XLA Modules:
  0.0 109.5 jit_solution(13193278079642665706)
XLA Ops:
  0.0 4.6 %prepare.1 = (f32[4,64,512]{2,1,0:T(8,128)}, f32[8,64,512]{2,1,0:T(8,128)}, f32[4,8,64,64]{3,2,1,0:T(8,128)}, s32[8,1,128]{2,1,0:T(1,128)}, s32[1,128]{1,0:T(1,128)}) custom-call(s32[1,8]{1,0:T(1,128)} %picked.1, s32[1,16]{1,0:T(1,128)} %owner.3, f32[4,8,4096]{2,1,0:T(8,128)} %prolong_raw.1, s32[4,8]{1,0:T(4,128)} %prolong_cols.1, s32[2,16]{1,0:T(2,128)} %pattern.1), custom_call_target="tpu_custom_call" | custom-call | tf_op jit(solution)/shard_map/prepare/pallas_call | solution.py:344
  4.6 44.3 %gather_rows.1 = (f32[24,64,512]{2,1,0:T(8,128)}, s32[12,1,128]{2,1,0:T(1,128)}, f32[4,16,64,64]{3,2,1,0:T(8,128)}) custom-call(f32[4,64,512]{2,1,0:T(8,128)} %get-tuple-element.13.panels, f32[8,64,512]{2,1,0:T(8,128)} %get-tuple-element.14.outgoing, s32[8,1,128]{2,1,0:T(1,128)} %get-tuple-element.15.dom_meta, s32[1,128]{1,0:T(1,128)} %get-tuple-element.16.grp_meta, ...), custom_call_target="tpu_custom_call" | custom-call | tf_op jit(solution)/shard_map/gather_rows/pallas_call | solution.py:356
  48.9 1.3 %copy.13 = s32[12,1,128]{2,0,1:T(8,128)} copy(s32[12,1,128]{2,1,0:T(1,128)} %get-tuple-element.17) | data formatting | bytes 12288
  50.2 26.7 %block_products.1.packed = bf16[64,256,128]{2,1,0:T(8,128)(2,1)} custom-call(s32[4,16]{1,0:T(4,128)} %cols.1, s32[4]{0:T(128)} %halo.1, s32[12,128]{1,0:T(8,128)} %bitcast.7, f32[4,16,64,64]{3,2,1,0:T(8,128)} %get-tuple-element.18.operator, f32[24,64,512]{2,1,0:T(8,128)} %get-tuple-element.19.table), custom_call_target="tpu_custom_call" | custom-call | tf_op jit(solution)/shard_map/block_products/pallas_call | solution.py:374
  76.9 29.8 %sum_rows.1 = f32[2,64,1024]{2,1,0:T(8,128)} custom-call(s32[4,8]{1,0:T(4,128)} %slots.1, s32[1,16]{1,0:T(1,128)} %owner.3, s32[12,128]{1,0:T(8,128)} %bitcast.8, bf16[64,256,128]{2,1,0:T(8,128)(2,1)} %block_products.1.packed, f32[4,8,64,64]{3,2,1,0:T(8,128)} %get-tuple-element.20.prolong), custom_call_target="tpu_custom_call" | custom-call | tf_op jit(solution)/shard_map/sum_rows/pallas_call | solution.py:388
  106.8 1.3 %reshape.10 = f32[2,64,16,64]{3,2,1,0:T(8,128)S(1)} reshape(f32[2,64,1024]{2,1,0:T(8,128)} %sum_rows.1) | data formatting | bytes 1048576 | tf_op jit(solution)/shard_map/reshape | solution.py:403
  108.1 0.3 copy.10
  108.4 1.2 %reshape.11 = f32[2,16,4096]{2,1,0:T(8,128)} reshape(f32[2,16,64,64]{3,2,1,0:T(8,128)S(1)} %copy.10) | data formatting | bytes 1048576 | tf_op jit(solution)/shard_map/reshape | solution.py:403

commit v2 on v1

--- a/solution.py
+++ b/solution.py
@@ -27,9 +27,9 @@
 
 def gather_kernel(
     n_grp, n_dom, rows, hs,
-    panels, outgoing, dom_meta, grp_meta, operator,
-    table, meta, blocks,
-    own_sem, line_send, line_recv, dom_send, dom_recv, meta_send, meta_recv,
+    halo, panels, outgoing, dom_meta, grp_meta, operator,
+    table, meta, stacked,
+    blocks, own_sem, line_send, line_recv, dom_send, dom_recv, meta_send, meta_recv,
 ):
     g = lax.axis_index("grp")
     me = lax.axis_index("dom")
@@ -101,7 +101,17 @@
             blocks[i, :, a, :] = row[:, a * BS:(a + 1) * BS]
         return carry
 
+    def split_row(i, carry):
+        for m in range(blocks.shape[1]):
+            block = blocks[i, m]
+            if m >= KG:
+                block = jnp.where(m - KG < halo[i], block, 0.0)
+            high = block.astype(jnp.bfloat16).astype(jnp.float32)
+            stacked[i, m] = jnp.concatenate([high, high, block - high], axis=1).astype(jnp.bfloat16)
+        return carry
+
     lax.fori_loop(0, rows, relay_row, 0)
+    lax.fori_loop(0, rows, split_row, 0)
 
     def origin_of(direction, step):
         return g - 1 - step if direction == 0 else g + 1 + step
@@ -149,7 +159,7 @@
 
 def product_kernel(
     n_grp, n_dom, rows, hs, ka, kp,
-    cols, halo, meta,
+    cols, meta,
     operator, table,
     out,
     split_table, total,
@@ -176,44 +186,41 @@
 
         lax.fori_loop(0, panel_count, split, 0)
 
-        def pair(step, carry):
-            i = step // ka
-            m = step % ka
-            col = cols[i, m]
+        def pairs(m, carry):
             near = m < KG
-
-            @pl.when(near | (m - KG < halo[i]))
-            def _():
+            products = []
+            places = []
+            for i in range(rows):
+                col = cols[i, m]
                 panel = jnp.where(near, col, near_count + col)
                 meta_row = jnp.where(near, col // rows, n_grp + col // hs)
                 meta_lane = jnp.where(near, (col % rows) * kp, (col % hs) * kp)
-                high, low = split_pair(operator[i, m])
-                high = high.astype(jnp.float32)
-                low = low.astype(jnp.float32)
-                left = jnp.concatenate([high, high, low], axis=1).astype(jnp.bfloat16)
-                w = jnp.dot(left, split_table[panel], preferred_element_type=jnp.float32)
+                products.append(
+                    jnp.dot(operator[i, m], split_table[panel], preferred_element_type=jnp.float32)
+                )
+                places.append((meta_row, meta_lane))
+            for i in range(rows):
                 for q in range(0, kp, 2):
-                    piece = w[:, q * BS:(q + 2) * BS]
-                    first = meta[meta_row, meta_lane + q]
-                    second = meta[meta_row, meta_lane + q + 1]
-                    total[first, i] += jnp.where(lane, piece, 0.0)
-                    total[second, i] += jnp.where(lane, 0.0, piece)
-
+                    piece = products[i][:, q * BS:(q + 2) * BS]
+                    turned = pltpu.roll(piece, BS, 1)
+                    first = meta[places[i][0], 0, places[i][1] + q]
+                    second = meta[places[i][0], 0, places[i][1] + q + 1]
+                    total[first, i] += jnp.where(lane, piece, turned)
+                    total[second, i] += jnp.where(lane, turned, piece)
             return carry
 
-        lax.fori_loop(0, rows * ka, pair, 0)
+        lax.fori_loop(0, ka, pairs, 0)
 
     chunk = out.shape[0]
     half = lax.broadcasted_iota(jnp.int32, (rows * BS, LANES), 1) < BS
 
     def fold(t, carry):
         value = total[k * chunk + t].reshape(rows * BS, LANES)
-        value += pltpu.roll(value, BS, 1)
         high = value.astype(jnp.bfloat16).astype(jnp.float32)
         out[t] = jnp.where(half, high, value - high).astype(jnp.bfloat16)
         return carry
 
-    lax.fori_loop(0, chunk, fold, 0)
+    lax.fori_loop(0, chunk, fold, 0, unroll=4)
 
 
 def exchange_kernel(
@@ -243,7 +250,7 @@
         both = jnp.concatenate([left_high, left_low], axis=0)
         for c in range(0, kc, 2):
             right = jnp.concatenate(
-                [packed[meta[n_grp + owner_dom, pattern_at + c + h]] for h in range(2)], axis=1
+                [packed[meta[n_grp + owner_dom, 0, pattern_at + c + h]] for h in range(2)], axis=1
             )
             stacked = jnp.dot(both, right, preferred_element_type=jnp.float32)
             both_sum = stacked[:BS] + stacked[BS:]
@@ -253,27 +260,38 @@
                 folded.append(piece + pltpu.roll(piece, BS, 1))
             partial[at, :, c * BS:(c + 2) * BS] = jnp.where(lane, folded[0], folded[1])
 
+    assert n_dom & (n_dom - 1) == 0
+
+    def partner(k):
+        other = 0
+        bit = 1
+        while bit < n_dom:
+            other += lax.rem(me // bit + k // bit, 2) * bit
+            bit *= 2
+        return other
+
     def copy_of(k):
-        target = lax.rem(me + k, n_dom)
+        target = partner(k)
         return pltpu.make_async_remote_copy(
             src_ref=partial.at[k], dst_ref=arrived.at[k - 1],
             send_sem=send_sem.at[k - 1], recv_sem=recv_sem.at[k - 1],
             device_id={"dom": target},
         )
 
-    def far_slot(k, carry):
-        target = lax.rem(me + k, n_dom)
+    def far_slot(step, carry):
+        k = n_dom - step
+        target = partner(k)
         slot_rows(target, target * cap, k)
 
-        @pl.when(k > 1)
+        @pl.when(step > 1)
         def _():
-            copy_of(k - 1).start()
+            copy_of(k + 1).start()
 
         return carry
 
     lax.fori_loop(1, n_dom, far_slot, 0)
     slot_rows(me, me * cap, 0)
-    copy_of(n_dom - 1).start()
+    copy_of(1).start()
     owned = out.shape[0]
     for r in range(owned):
         out[r] = partial[0] * (owner[0, me * cap] == r).astype(jnp.float32)
@@ -281,10 +299,10 @@
         slot_rows(me, me * cap + t, n_dom + t - 1)
         for r in range(owned):
             out[r] += partial[n_dom + t - 1] * (owner[0, me * cap + t] == r).astype(jnp.float32)
-    for k in range(1, n_dom):
+    for k in range(n_dom - 1, 0, -1):
         copy_of(k).wait_recv()
-        source = lax.rem(me - k + n_dom, n_dom)
-        row = meta[n_grp + source, row_at]
+        source = partner(k)
+        row = meta[n_grp + source, 0, row_at]
         for r in range(owned):
             out[r] += arrived[k - 1] * (row == r).astype(jnp.float32)
     for k in range(1, n_dom):
@@ -353,21 +371,22 @@
     )(send_lists, slot_owner_row, prolong_blocks, prolong_cols, coarse_pattern)
 
     sem = pltpu.SemaphoreType.DMA
-    table, meta, blocks = pl.pallas_call(
+    table, meta, stacked = pl.pallas_call(
         functools.partial(gather_kernel, n_grp, n_dom, rows, hs),
         out_shape=(
-            f32(panel_count, BS, kp * BS), i32(n_grp + n_dom, 1, LANES), f32(rows, ka, BS, BS),
+            f32(panel_count, BS, kp * BS), i32(n_grp + n_dom, 1, LANES),
+            jax.ShapeDtypeStruct((rows, ka, BS, 3 * BS), jnp.bfloat16),
         ),
-        in_specs=[vmem_spec()] * 5,
+        in_specs=[smem_spec()] + [vmem_spec()] * 5,
         out_specs=(any_spec(), any_spec(), vmem_spec()),
         scratch_shapes=[
+            pltpu.VMEM((rows, ka, BS, BS), jnp.float32),
             sem((4,)), sem((2, n_grp - 1, rows)), sem((2, n_grp - 1, rows)),
             sem((n_dom,)), sem((n_dom,)), sem((n_grp + n_dom,)), sem((n_grp + n_dom,)),
         ],
         compiler_params=pltpu.CompilerParams(collective_id=0, has_side_effects=True),
         name="gather_rows",
-    )(panels, outgoing, dom_meta, grp_meta, operator_blocks)
-    meta = meta.reshape(n_grp + n_dom, LANES)
+    )(halo_count, panels, outgoing, dom_meta, grp_meta, operator_blocks)
 
     whole = lambda shape: pl.BlockSpec(shape, lambda k: (0,) * len(shape), pipeline_mode=pl.Buffered(1))
     chunk = 8
@@ -375,7 +394,7 @@
         functools.partial(product_kernel, n_grp, n_dom, rows, hs, ka, kp),
         grid=(total_ids // chunk,),
         out_shape=jax.ShapeDtypeStruct((total_ids, rows * BS, LANES), jnp.bfloat16),
-        in_specs=[smem_spec()] * 3 + [whole((rows, ka, BS, BS)), whole((panel_count, BS, kp * BS))],
+        in_specs=[smem_spec()] * 2 + [whole((rows, ka, BS, 3 * BS)), whole((panel_count, BS, kp * BS))],
         out_specs=pl.BlockSpec((chunk, rows * BS, LANES), lambda k: (k, 0, 0)),
         scratch_shapes=[
             pltpu.VMEM((panel_count, 3 * BS, kp * BS), jnp.bfloat16),
@@ -383,7 +402,7 @@
         ],
         compiler_params=pltpu.CompilerParams(vmem_limit_bytes=63000 * 1024),
         name="block_products",
-    )(operator_cols, halo_count, meta, blocks, table)
+    )(operator_cols, meta, stacked, table)
 
     summed = pl.pallas_call(
         functools.partial(exchange_kernel, n_grp, n_dom, rows, hs, kp, kc, cap, row_at),

time: 110 us -> 98.5 us (0.90)
  Pallas kernels: 105 us -> 95.5 us
  local copies, waits for them, and re-layouts: 4.07 us -> 2.78 us
    pallas_call x1, Pallas kernels: 26.7 us -> 15.3 us  [per_device(): pl.pallas_call(functools.partial(product_kernel, n_grp, n_dom, rows, hs,...]
    pallas_call x1, Pallas kernels: 29.8 us -> 31.2 us  [per_device(): pl.pallas_call(functools.partial(exchange_kernel, n_grp, n_dom, rows, hs,...]
    unnamed x1 -> x0, local copies, waits for them, and re-layouts: 1.29 us -> none
where the time goes in v2:
time: 98.5 us; the launch traced here: 98.3 us
  Pallas kernels  95.5 us (97%)
  local copies, waits for them, and re-layouts  2.78 us (3%)
    pallas_call x1, Pallas kernels, per_device(): pl.pallas_call(functools.partial(gather_kernel, n_grp, n_dom, rows, hs),...  44.4 us
    pallas_call x1, Pallas kernels, per_device(): pl.pallas_call(functools.partial(exchange_kernel, n_grp, n_dom, rows, hs,...  31.2 us
    pallas_call x1, Pallas kernels, per_device(): pl.pallas_call(functools.partial(product_kernel, n_grp, n_dom, rows, hs,...  15.3 us
    pallas_call x1, Pallas kernels, per_device(): pl.pallas_call(functools.partial(prepare_kernel, n_dom, rows, hs, kp, kc,...  4.59 us
    reshape x2, local copies, waits for them, and re-layouts, per_device(): summed.reshape(owned, BS, kc, BS).transpose(0, 2, 1, 3)  2.46 us

profile of v2, /device:TPU:0, one launch (start us, length us, event | category | flops | bytes accessed | tf_op | source)
XLA Modules:
  0.0 98.3 jit_solution(4773200697745939116)
XLA Ops:
  0.0 4.6 %prepare.1 = (f32[4,64,512]{2,1,0:T(8,128)}, f32[8,64,512]{2,1,0:T(8,128)}, f32[4,8,64,64]{3,2,1,0:T(8,128)}, s32[8,1,128]{2,1,0:T(1,128)}, s32[1,128]{1,0:T(1,128)}) custom-call(s32[1,8]{1,0:T(1,128)} %picked.1, s32[1,16]{1,0:T(1,128)} %owner.3, f32[4,8,4096]{2,1,0:T(8,128)} %prolong_raw.1, s32[4,8]{1,0:T(4,128)} %prolong_cols.1, s32[2,16]{1,0:T(2,128)} %pattern.1), custom_call_target="tpu_custom_call" | custom-call | tf_op jit(solution)/shard_map/prepare/pallas_call | solution.py:362
  4.6 44.4 %gather_rows.1 = (f32[24,64,512]{2,1,0:T(8,128)}, s32[12,1,128]{2,1,0:T(1,128)}, bf16[4,16,64,192]{3,2,1,0:T(8,128)(2,1)}) custom-call(s32[4]{0:T(128)} %halo.1, f32[4,64,512]{2,1,0:T(8,128)} %get-tuple-element.13.panels, f32[8,64,512]{2,1,0:T(8,128)} %get-tuple-element.14.outgoing, s32[8,1,128]{2,1,0:T(1,128)} %get-tuple-element.15.dom_meta, ...), custom_call_target="tpu_custom_call" | custom-call | tf_op jit(solution)/shard_map/gather_rows/pallas_call | solution.py:374
  49.0 15.3 %block_products.1.packed = bf16[64,256,128]{2,1,0:T(8,128)(2,1)} custom-call(s32[4,16]{1,0:T(4,128)} %cols.1, s32[12,1,128]{2,1,0:T(1,128)} %get-tuple-element.17.meta, bf16[4,16,64,192]{3,2,1,0:T(8,128)(2,1)} %get-tuple-element.18.operator, f32[24,64,512]{2,1,0:T(8,128)} %get-tuple-element.19.table), custom_call_target="tpu_custom_call" | custom-call | tf_op jit(solution)/shard_map/block_products/pallas_call | solution.py:393
  64.3 31.2 %sum_rows.1 = f32[2,64,1024]{2,1,0:T(8,128)} custom-call(s32[4,8]{1,0:T(4,128)} %slots.1, s32[1,16]{1,0:T(1,128)} %owner.3, s32[12,1,128]{2,1,0:T(1,128)} %get-tuple-element.17.meta, bf16[64,256,128]{2,1,0:T(8,128)(2,1)} %block_products.1.packed, f32[4,8,64,64]{3,2,1,0:T(8,128)} %get-tuple-element.20.prolong), custom_call_target="tpu_custom_call" | custom-call | tf_op jit(solution)/shard_map/sum_rows/pallas_call | solution.py:407
  95.5 1.3 %reshape.6 = f32[2,64,16,64]{3,2,1,0:T(8,128)S(1)} reshape(f32[2,64,1024]{2,1,0:T(8,128)} %sum_rows.1) | data formatting | bytes 1048576 | tf_op jit(solution)/shard_map/reshape | solution.py:422
  96.8 0.3 copy.10
  97.1 1.2 %reshape.7 = f32[2,16,4096]{2,1,0:T(8,128)} reshape(f32[2,16,64,64]{3,2,1,0:T(8,128)S(1)} %copy.10) | data formatting | bytes 1048576 | tf_op jit(solution)/shard_map/reshape | solution.py:422

commit v3 on v2

--- a/solution.py
+++ b/solution.py
@@ -25,11 +25,43 @@
     return pl.BlockSpec(memory_space=pltpu.SMEM)
 
 
+def prepare_rows(
+    n_dom, rows, hs, kp, kc, cap,
+    picked, owner, prolong_raw, prolong_cols, pattern,
+    panels, outgoing, prolong, dom_meta, grp_meta,
+):
+    owned = pattern.shape[0]
+    for i in range(rows):
+        raw = prolong_raw[i]
+        for a in range(BS):
+            prolong[i, :, a, :] = raw[:, a * BS:(a + 1) * BS]
+        for q in range(0, kp, 2):
+            panels[i, :, q * BS:(q + 2) * BS] = jnp.concatenate([prolong[i, q], prolong[i, q + 1]], axis=1)
+    grp_meta[...] = jnp.zeros(grp_meta.shape, jnp.int32)
+    dom_meta[...] = jnp.zeros(dom_meta.shape, jnp.int32)
+    for i in range(rows):
+        grp_meta[:, i * kp:(i + 1) * kp] = prolong_cols[i:i + 1, :]
+    row_at = hs * kp + owned * kc
+
+    def for_dom(d, carry):
+        for h in range(hs):
+            row = picked[0, d * hs + h]
+            outgoing[d * hs + h] = panels[row]
+            dom_meta[d, :, h * kp:(h + 1) * kp] = prolong_cols[pl.ds(row, 1), :]
+        for r in range(owned):
+            at = hs * kp + r * kc
+            dom_meta[d, :, at:at + kc] = pattern[r:r + 1, :]
+        dom_meta[d, :, row_at:row_at + 1] = jnp.full((1, 1), owner[0, d * cap], jnp.int32)
+        return carry
+
+    lax.fori_loop(0, n_dom, for_dom, 0)
+
+
 def gather_kernel(
-    n_grp, n_dom, rows, hs,
-    halo, panels, outgoing, dom_meta, grp_meta, operator,
-    table, meta, stacked,
-    blocks, own_sem, line_send, line_recv, dom_send, dom_recv, meta_send, meta_recv,
+    n_grp, n_dom, rows, hs, kp, kc, cap,
+    halo, picked, owner, prolong_raw, prolong_cols, pattern, operator,
+    table, meta, stacked, prolong,
+    panels, outgoing, dom_meta, grp_meta, blocks, own_sem, line_send, line_recv, dom_send, dom_recv, meta_send, meta_recv,
 ):
     g = lax.axis_index("grp")
     me = lax.axis_index("dom")
@@ -39,6 +71,11 @@
         pl.semaphore_signal(barrier, inc=1, device_id={"grp": lax.rem(g + k, n_grp)})
     for k in range(1, n_dom):
         pl.semaphore_signal(barrier, inc=1, device_id={"dom": lax.rem(me + k, n_dom)})
+    prepare_rows(
+        n_dom, rows, hs, kp, kc, cap,
+        picked, owner, prolong_raw, prolong_cols, pattern,
+        panels, outgoing, prolong, dom_meta, grp_meta,
+    )
     pl.semaphore_wait(barrier, n_grp + n_dom - 2)
 
     def line_copy(direction, step, r, src, origin):
@@ -227,7 +264,7 @@
     n_grp, n_dom, rows, hs, kp, kc, cap, row_at,
     slots, owner, meta, packed, prolong,
     out,
-    partial, arrived, send_sem, recv_sem,
+    partial, arrived, summed, send_sem, recv_sem,
 ):
     me = lax.axis_index("dom")
     barrier = pltpu.get_barrier_semaphore()
@@ -294,51 +331,22 @@
     copy_of(1).start()
     owned = out.shape[0]
     for r in range(owned):
-        out[r] = partial[0] * (owner[0, me * cap] == r).astype(jnp.float32)
+        summed[r] = partial[0] * (owner[0, me * cap] == r).astype(jnp.float32)
     for t in range(1, cap):
         slot_rows(me, me * cap + t, n_dom + t - 1)
         for r in range(owned):
-            out[r] += partial[n_dom + t - 1] * (owner[0, me * cap + t] == r).astype(jnp.float32)
+            summed[r] += partial[n_dom + t - 1] * (owner[0, me * cap + t] == r).astype(jnp.float32)
     for k in range(n_dom - 1, 0, -1):
         copy_of(k).wait_recv()
         source = partner(k)
         row = meta[n_grp + source, 0, row_at]
         for r in range(owned):
-            out[r] += arrived[k - 1] * (row == r).astype(jnp.float32)
+            summed[r] += arrived[k - 1] * (row == r).astype(jnp.float32)
+    for r in range(owned):
+        for c in range(kc):
+            out[r, c] = summed[r, :, c * BS:(c + 1) * BS]
     for k in range(1, n_dom):
         copy_of(k).wait_send()
-
-
-def prepare_kernel(
-    n_dom, rows, hs, kp, kc, cap,
-    picked, owner, prolong_raw, prolong_cols, pattern,
-    panels, outgoing, prolong, dom_meta, grp_meta,
-):
-    owned = pattern.shape[0]
-    for i in range(rows):
-        raw = prolong_raw[i]
-        for a in range(BS):
-            prolong[i, :, a, :] = raw[:, a * BS:(a + 1) * BS]
-        for q in range(0, kp, 2):
-            panels[i, :, q * BS:(q + 2) * BS] = jnp.concatenate([prolong[i, q], prolong[i, q + 1]], axis=1)
-    grp_meta[...] = jnp.zeros(grp_meta.shape, jnp.int32)
-    dom_meta[...] = jnp.zeros(dom_meta.shape, jnp.int32)
-    for i in range(rows):
-        grp_meta[:, i * kp:(i + 1) * kp] = prolong_cols[i:i + 1, :]
-    row_at = hs * kp + owned * kc
-
-    def for_dom(d, carry):
-        for h in range(hs):
-            row = picked[0, d * hs + h]
-            outgoing[d * hs + h] = panels[row]
-            dom_meta[d, :, h * kp:(h + 1) * kp] = prolong_cols[pl.ds(row, 1), :]
-        for r in range(owned):
-            at = hs * kp + r * kc
-            dom_meta[d, :, at:at + kc] = pattern[r:r + 1, :]
-        dom_meta[d, :, row_at:row_at + 1] = jnp.full((1, 1), owner[0, d * cap], jnp.int32)
-        return carry
-
-    lax.fori_loop(0, n_dom, for_dom, 0)
 
 
 def per_device(
@@ -359,34 +367,29 @@
     f32 = lambda *shape: jax.ShapeDtypeStruct(shape, jnp.float32)
     i32 = lambda *shape: jax.ShapeDtypeStruct(shape, jnp.int32)
 
-    panels, outgoing, prolong, dom_meta, grp_meta = pl.pallas_call(
-        functools.partial(prepare_kernel, n_dom, rows, hs, kp, kc, cap),
-        out_shape=(
-            f32(rows, BS, kp * BS), f32(n_dom * hs, BS, kp * BS), f32(rows, kp, BS, BS),
-            i32(n_dom, 1, LANES), i32(1, LANES),
-        ),
-        in_specs=[smem_spec()] * 2 + [vmem_spec()] * 3,
-        out_specs=(vmem_spec(),) * 5,
-        name="prepare",
-    )(send_lists, slot_owner_row, prolong_blocks, prolong_cols, coarse_pattern)
-
     sem = pltpu.SemaphoreType.DMA
-    table, meta, stacked = pl.pallas_call(
-        functools.partial(gather_kernel, n_grp, n_dom, rows, hs),
+    table, meta, stacked, prolong = pl.pallas_call(
+        functools.partial(gather_kernel, n_grp, n_dom, rows, hs, kp, kc, cap),
         out_shape=(
             f32(panel_count, BS, kp * BS), i32(n_grp + n_dom, 1, LANES),
-            jax.ShapeDtypeStruct((rows, ka, BS, 3 * BS), jnp.bfloat16),
+            jax.ShapeDtypeStruct((rows, ka, BS, 3 * BS), jnp.bfloat16), f32(rows, kp, BS, BS),
         ),
-        in_specs=[smem_spec()] + [vmem_spec()] * 5,
-        out_specs=(any_spec(), any_spec(), vmem_spec()),
+        in_specs=[smem_spec()] * 3 + [vmem_spec()] * 4,
+        out_specs=(any_spec(), any_spec(), vmem_spec(), vmem_spec()),
         scratch_shapes=[
+            pltpu.VMEM((rows, BS, kp * BS), jnp.float32),
+            pltpu.VMEM((n_dom * hs, BS, kp * BS), jnp.float32),
+            pltpu.VMEM((n_dom, 1, LANES), jnp.int32),
+            pltpu.VMEM((1, LANES), jnp.int32),
             pltpu.VMEM((rows, ka, BS, BS), jnp.float32),
             sem((4,)), sem((2, n_grp - 1, rows)), sem((2, n_grp - 1, rows)),
             sem((n_dom,)), sem((n_dom,)), sem((n_grp + n_dom,)), sem((n_grp + n_dom,)),
         ],
         compiler_params=pltpu.CompilerParams(collective_id=0, has_side_effects=True),
         name="gather_rows",
-    )(halo_count, panels, outgoing, dom_meta, grp_meta, operator_blocks)
+    )(
+        halo_count, send_lists, slot_owner_row, prolong_blocks, prolong_cols, coarse_pattern, operator_blocks
+    )
 
     whole = lambda shape: pl.BlockSpec(shape, lambda k: (0,) * len(shape), pipeline_mode=pl.Buffered(1))
     chunk = 8
@@ -406,12 +409,13 @@
 
     summed = pl.pallas_call(
         functools.partial(exchange_kernel, n_grp, n_dom, rows, hs, kp, kc, cap, row_at),
-        out_shape=f32(owned, BS, kc * BS),
+        out_shape=f32(owned, kc, BS, BS),
         in_specs=[smem_spec()] * 3 + [vmem_spec()] * 2,
         out_specs=vmem_spec(),
         scratch_shapes=[
             pltpu.VMEM((used, BS, kc * BS), jnp.float32),
             pltpu.VMEM((n_dom - 1, BS, kc * BS), jnp.float32),
+            pltpu.VMEM((owned, BS, kc * BS), jnp.float32),
             sem((n_dom - 1,)), sem((n_dom - 1,)),
         ],
         compiler_params=pltpu.CompilerParams(
@@ -419,7 +423,7 @@
         ),
         name="sum_rows",
     )(prolong_slot, slot_owner_row, meta, packed, prolong)
-    return summed.reshape(owned, BS, kc, BS).transpose(0, 2, 1, 3).reshape(owned, kc, BS * BS)
+    return summed.reshape(owned, kc, BS * BS)
 
 
 def solution(mesh):

time: 98.5 us -> 93.9 us (0.953)
  Pallas kernels: 95.5 us -> 91.4 us
    pallas_call x2 -> x1, Pallas kernels: 48.9 us -> 44.4 us  [per_device(): pl.pallas_call(functools.partial(gather_kernel, n_grp, n_dom, rows, hs, k...]
    reshape x2 -> x1, local copies, waits for them, and re-layouts: 2.46 us -> 2.37 us  [per_device(): return summed.reshape(owned, kc, BS * BS)]
where the time goes in v3:
time: 93.9 us; the launch traced here: 93.8 us
  Pallas kernels  91.4 us (97%)
  local copies, waits for them, and re-layouts  2.37 us (3%)
    pallas_call x1, Pallas kernels, per_device(): pl.pallas_call(functools.partial(gather_kernel, n_grp, n_dom, rows, hs, k...  44.4 us
    pallas_call x1, Pallas kernels, per_device(): pl.pallas_call(functools.partial(exchange_kernel, n_grp, n_dom, rows, hs,...  31.6 us
    pallas_call x1, Pallas kernels, per_device(): pl.pallas_call(functools.partial(product_kernel, n_grp, n_dom, rows, hs,...  15.4 us
    reshape x1, local copies, waits for them, and re-layouts, per_device(): return summed.reshape(owned, kc, BS * BS)  2.37 us

profile of v3, /device:TPU:0, one launch (start us, length us, event | category | flops | bytes accessed | tf_op | source)
XLA Modules:
  0.0 93.8 jit_solution(18064334782393434458)
XLA Ops:
  0.0 44.4 %gather_rows.1 = (f32[24,64,512]{2,1,0:T(8,128)}, s32[12,1,128]{2,1,0:T(1,128)}, bf16[4,16,64,192]{3,2,1,0:T(8,128)(2,1)}, f32[4,8,64,64]{3,2,1,0:T(8,128)}) custom-call(s32[4]{0:T(128)} %halo.1, s32[1,8]{1,0:T(1,128)} %picked.1, s32[1,16]{1,0:T(1,128)} %owner.3, f32[4,8,4096]{2,1,0:T(8,128)} %prolong_raw.1, s32[4,8]{1,0:T(4,128)} %prolong_cols.1, ...), custom_call_target="tpu_custom_call" | custom-call | tf_op jit(solution)/shard_map/gather_rows/pallas_call | solution.py:371
  44.4 15.4 %block_products.1.packed = bf16[64,256,128]{2,1,0:T(8,128)(2,1)} custom-call(s32[4,16]{1,0:T(4,128)} %cols.1, s32[12,1,128]{2,1,0:T(1,128)} %get-tuple-element.9.meta, bf16[4,16,64,192]{3,2,1,0:T(8,128)(2,1)} %get-tuple-element.10.operator, f32[24,64,512]{2,1,0:T(8,128)} %get-tuple-element.11.table), custom_call_target="tpu_custom_call" | custom-call | tf_op jit(solution)/shard_map/block_products/pallas_call | solution.py:396
  59.8 31.6 %sum_rows.1 = f32[2,16,64,64]{3,2,1,0:T(8,128)} custom-call(s32[4,8]{1,0:T(4,128)} %slots.1, s32[1,16]{1,0:T(1,128)} %owner.3, s32[12,1,128]{2,1,0:T(1,128)} %get-tuple-element.9.meta, bf16[64,256,128]{2,1,0:T(8,128)(2,1)} %block_products.1.packed, f32[4,8,64,64]{3,2,1,0:T(8,128)} %get-tuple-element.12.prolong), custom_call_target="tpu_custom_call" | custom-call | tf_op jit(solution)/shard_map/sum_rows/pallas_call | solution.py:410
  91.4 2.4 %reshape.3 = f32[2,16,4096]{2,1,0:T(8,128)} reshape(f32[2,16,64,64]{3,2,1,0:T(8,128)} %sum_rows.1) | data formatting | bytes 1048576 | tf_op jit(solution)/shard_map/reshape | solution.py:426

commit v4 on v3

--- a/solution.py
+++ b/solution.py
@@ -59,8 +59,9 @@
 
 def gather_kernel(
     n_grp, n_dom, rows, hs, kp, kc, cap,
-    halo, picked, owner, prolong_raw, prolong_cols, pattern, operator,
-    table, meta, stacked, prolong,
+    halo, picked, owner, prolong_raw, prolong_cols, pattern, operator_in,
+    table, meta, stacked_out, prolong_out,
+    operator, stacked, prolong, bulk_sem,
     panels, outgoing, dom_meta, grp_meta, blocks, own_sem, line_send, line_recv, dom_send, dom_recv, meta_send, meta_recv,
 ):
     g = lax.axis_index("grp")
@@ -71,6 +72,8 @@
         pl.semaphore_signal(barrier, inc=1, device_id={"grp": lax.rem(g + k, n_grp)})
     for k in range(1, n_dom):
         pl.semaphore_signal(barrier, inc=1, device_id={"dom": lax.rem(me + k, n_dom)})
+    operator_copy = pltpu.make_async_copy(operator_in, operator, bulk_sem.at[0])
+    operator_copy.start()
     prepare_rows(
         n_dom, rows, hs, kp, kc, cap,
         picked, owner, prolong_raw, prolong_cols, pattern,
@@ -147,8 +150,13 @@
             stacked[i, m] = jnp.concatenate([high, high, block - high], axis=1).astype(jnp.bfloat16)
         return carry
 
+    prolong_copy = pltpu.make_async_copy(prolong, prolong_out, bulk_sem.at[1])
+    stacked_copy = pltpu.make_async_copy(stacked, stacked_out, bulk_sem.at[2])
+    prolong_copy.start()
+    operator_copy.wait()
     lax.fori_loop(0, rows, relay_row, 0)
     lax.fori_loop(0, rows, split_row, 0)
+    stacked_copy.start()
 
     def origin_of(direction, step):
         return g - 1 - step if direction == 0 else g + 1 + step
@@ -170,6 +178,8 @@
                         src = table.at[origin * rows + r]
                         line_copy(direction, step + 1, r, src, origin).start()
 
+    prolong_copy.wait()
+    stacked_copy.wait()
     for copy in own:
         copy.wait()
     for k in range(1, n_grp):
@@ -197,9 +207,9 @@
 def product_kernel(
     n_grp, n_dom, rows, hs, ka, kp,
     cols, meta,
-    operator, table,
+    operator_in, table_in,
     out,
-    split_table, total,
+    operator, table, split_table, total, load_sem,
 ):
     k = pl.program_id(0)
     panel_count = table.shape[0]
@@ -208,6 +218,11 @@
 
     @pl.when(k == 0)
     def _():
+        table_copy = pltpu.make_async_copy(table_in, table, load_sem.at[0])
+        operator_copy = pltpu.make_async_copy(operator_in, operator, load_sem.at[1])
+        table_copy.start()
+        operator_copy.start()
+
         def clear(e, carry):
             total[e] = jnp.zeros(total.shape[1:], jnp.float32)
             return carry
@@ -221,7 +236,9 @@
             split_table[p, 2 * BS:3 * BS] = high
             return carry
 
+        table_copy.wait()
         lax.fori_loop(0, panel_count, split, 0)
+        operator_copy.wait()
 
         def pairs(m, carry):
             near = m < KG
@@ -262,15 +279,23 @@
 
 def exchange_kernel(
     n_grp, n_dom, rows, hs, kp, kc, cap, row_at,
-    slots, owner, meta, packed, prolong,
+    slots, owner, meta, packed_in, prolong_in,
     out,
-    partial, arrived, summed, send_sem, recv_sem,
+    packed, prolong, load_sem, partial, arrived, summed, send_sem, recv_sem,
 ):
     me = lax.axis_index("dom")
+    loads = (
+        pltpu.make_async_copy(packed_in, packed, load_sem.at[0]),
+        pltpu.make_async_copy(prolong_in, prolong, load_sem.at[1]),
+    )
+    for load in loads:
+        load.start()
     barrier = pltpu.get_barrier_semaphore()
     for k in range(1, n_dom):
         pl.semaphore_signal(barrier, inc=1, device_id={"dom": lax.rem(me + k, n_dom)})
     pl.semaphore_wait(barrier, n_dom - 1)
+    for load in loads:
+        load.wait()
     lane = lax.broadcasted_iota(jnp.int32, (BS, LANES), 1) < BS
 
     def slot_rows(owner_dom, slot, at):
@@ -374,9 +399,13 @@
             f32(panel_count, BS, kp * BS), i32(n_grp + n_dom, 1, LANES),
             jax.ShapeDtypeStruct((rows, ka, BS, 3 * BS), jnp.bfloat16), f32(rows, kp, BS, BS),
         ),
-        in_specs=[smem_spec()] * 3 + [vmem_spec()] * 4,
-        out_specs=(any_spec(), any_spec(), vmem_spec(), vmem_spec()),
+        in_specs=[smem_spec()] * 3 + [vmem_spec()] * 3 + [any_spec()],
+        out_specs=(any_spec(),) * 4,
         scratch_shapes=[
+            pltpu.VMEM((rows, ka, BS * BS), jnp.float32),
+            pltpu.VMEM((rows, ka, BS, 3 * BS), jnp.bfloat16),
+            pltpu.VMEM((rows, kp, BS, BS), jnp.float32),
+            sem((3,)),
             pltpu.VMEM((rows, BS, kp * BS), jnp.float32),
             pltpu.VMEM((n_dom * hs, BS, kp * BS), jnp.float32),
             pltpu.VMEM((n_dom, 1, LANES), jnp.int32),
@@ -391,17 +420,19 @@
         halo_count, send_lists, slot_owner_row, prolong_blocks, prolong_cols, coarse_pattern, operator_blocks
     )
 
-    whole = lambda shape: pl.BlockSpec(shape, lambda k: (0,) * len(shape), pipeline_mode=pl.Buffered(1))
     chunk = 8
     packed = pl.pallas_call(
         functools.partial(product_kernel, n_grp, n_dom, rows, hs, ka, kp),
         grid=(total_ids // chunk,),
         out_shape=jax.ShapeDtypeStruct((total_ids, rows * BS, LANES), jnp.bfloat16),
-        in_specs=[smem_spec()] * 2 + [whole((rows, ka, BS, 3 * BS)), whole((panel_count, BS, kp * BS))],
+        in_specs=[smem_spec()] * 2 + [any_spec()] * 2,
         out_specs=pl.BlockSpec((chunk, rows * BS, LANES), lambda k: (k, 0, 0)),
         scratch_shapes=[
+            pltpu.VMEM((rows, ka, BS, 3 * BS), jnp.bfloat16),
+            pltpu.VMEM((panel_count, BS, kp * BS), jnp.float32),
             pltpu.VMEM((panel_count, 3 * BS, kp * BS), jnp.bfloat16),
             pltpu.VMEM((total_ids, rows, BS, LANES), jnp.float32),
+            sem((2,)),
         ],
         compiler_params=pltpu.CompilerParams(vmem_limit_bytes=63000 * 1024),
         name="block_products",
@@ -410,9 +441,12 @@
     summed = pl.pallas_call(
         functools.partial(exchange_kernel, n_grp, n_dom, rows, hs, kp, kc, cap, row_at),
         out_shape=f32(owned, kc, BS, BS),
-        in_specs=[smem_spec()] * 3 + [vmem_spec()] * 2,
+        in_specs=[smem_spec()] * 3 + [any_spec()] * 2,
         out_specs=vmem_spec(),
         scratch_shapes=[
+            pltpu.VMEM((total_ids, rows * BS, LANES), jnp.bfloat16),
+            pltpu.VMEM((rows, kp, BS, BS), jnp.float32),
+            sem((2,)),
             pltpu.VMEM((used, BS, kc * BS), jnp.float32),
             pltpu.VMEM((n_dom - 1, BS, kc * BS), jnp.float32),
             pltpu.VMEM((owned, BS, kc * BS), jnp.float32),

time: 93.9 us -> 90.4 us (0.963)
  Pallas kernels: 91.4 us -> 87.7 us
    pallas_call x1, Pallas kernels: 44.4 us -> 42.4 us  [per_device(): pl.pallas_call(functools.partial(gather_kernel, n_grp, n_dom, rows, hs, k...]
    pallas_call x1, Pallas kernels: 31.6 us -> 30.3 us  [per_device(): pl.pallas_call(functools.partial(exchange_kernel, n_grp, n_dom, rows, hs,...]
where the time goes in v4:
time: 90.4 us; the launch traced here: 90.1 us
  Pallas kernels  87.7 us (97%)
  local copies, waits for them, and re-layouts  2.37 us (3%)
    pallas_call x1, Pallas kernels, per_device(): pl.pallas_call(functools.partial(gather_kernel, n_grp, n_dom, rows, hs, k...  42.4 us
    pallas_call x1, Pallas kernels, per_device(): pl.pallas_call(functools.partial(exchange_kernel, n_grp, n_dom, rows, hs,...  30.3 us
    pallas_call x1, Pallas kernels, per_device(): pl.pallas_call(functools.partial(product_kernel, n_grp, n_dom, rows, hs,...  15.1 us
    reshape x1, local copies, waits for them, and re-layouts, per_device(): return summed.reshape(owned, kc, BS * BS)  2.37 us

profile of v4, /device:TPU:0, one launch (start us, length us, event | category | flops | bytes accessed | tf_op | source)
XLA Modules:
  0.0 90.1 jit_solution(15927454183014102317)
XLA Ops:
  0.0 42.4 %gather_rows.1 = (f32[24,64,512]{2,1,0:T(8,128)}, s32[12,1,128]{2,1,0:T(1,128)}, bf16[4,16,64,192]{3,2,1,0:T(8,128)(2,1)}, f32[4,8,64,64]{3,2,1,0:T(8,128)}) custom-call(s32[4]{0:T(128)} %halo.1, s32[1,8]{1,0:T(1,128)} %picked.1, s32[1,16]{1,0:T(1,128)} %owner.3, f32[4,8,4096]{2,1,0:T(8,128)} %prolong_raw.1, s32[4,8]{1,0:T(4,128)} %prolong_cols.1, ...), custom_call_target="tpu_custom_call" | custom-call | tf_op jit(solution)/shard_map/gather_rows/pallas_call | solution.py:396
  42.4 15.1 %block_products.1.packed_in = bf16[64,256,128]{2,1,0:T(8,128)(2,1)} custom-call(s32[4,16]{1,0:T(4,128)} %cols.1, s32[12,1,128]{2,1,0:T(1,128)} %get-tuple-element.9.meta, bf16[4,16,64,192]{3,2,1,0:T(8,128)(2,1)} %get-tuple-element.10.operator_in, f32[24,64,512]{2,1,0:T(8,128)} %get-tuple-element.11.table_in), custom_call_target="tpu_custom_call" | custom-call | tf_op jit(solution)/shard_map/block_products/pallas_call | solution.py:424
  57.4 30.3 %sum_rows.1 = f32[2,16,64,64]{3,2,1,0:T(8,128)} custom-call(s32[4,8]{1,0:T(4,128)} %slots.1, s32[1,16]{1,0:T(1,128)} %owner.3, s32[12,1,128]{2,1,0:T(1,128)} %get-tuple-element.9.meta, bf16[64,256,128]{2,1,0:T(8,128)(2,1)} %block_products.1.packed_in, f32[4,8,64,64]{3,2,1,0:T(8,128)} %get-tuple-element.12.prolong_in), custom_call_target="tpu_custom_call" | custom-call | tf_op jit(solution)/shard_map/sum_rows/pallas_call | solution.py:441
  87.7 2.4 %reshape.3 = f32[2,16,4096]{2,1,0:T(8,128)} reshape(f32[2,16,64,64]{3,2,1,0:T(8,128)} %sum_rows.1) | data formatting | bytes 1048576 | tf_op jit(solution)/shard_map/reshape | solution.py:460

commit v5 on v4

--- a/solution.py
+++ b/solution.py
@@ -254,13 +254,17 @@
                 )
                 places.append((meta_row, meta_lane))
             for i in range(rows):
-                for q in range(0, kp, 2):
-                    piece = products[i][:, q * BS:(q + 2) * BS]
-                    turned = pltpu.roll(piece, BS, 1)
-                    first = meta[places[i][0], 0, places[i][1] + q]
-                    second = meta[places[i][0], 0, places[i][1] + q + 1]
-                    total[first, i] += jnp.where(lane, piece, turned)
-                    total[second, i] += jnp.where(lane, turned, piece)
+                for start in range(0, kp, 4):
+                    updates = []
+                    for q in range(start, min(start + 4, kp), 2):
+                        piece = products[i][:, q * BS:(q + 2) * BS]
+                        turned = pltpu.roll(piece, BS, 1)
+                        first = meta[places[i][0], 0, places[i][1] + q]
+                        second = meta[places[i][0], 0, places[i][1] + q + 1]
+                        updates.append((first, total[first, i] + jnp.where(lane, piece, turned)))
+                        updates.append((second, total[second, i] + jnp.where(lane, turned, piece)))
+                    for place, value in updates:
+                        total[place, i] = value
             return carry
 
         lax.fori_loop(0, ka, pairs, 0)

time: 90.4 us -> 89.8 us (level)
  no operation moved by 1% of the time
where the time goes in v5:
time: 89.8 us; the launch traced here: 89.5 us
  Pallas kernels  87.1 us (97%)
  local copies, waits for them, and re-layouts  2.37 us (3%)
    pallas_call x1, Pallas kernels, per_device(): pl.pallas_call(functools.partial(gather_kernel, n_grp, n_dom, rows, hs, k...  42.4 us
    pallas_call x1, Pallas kernels, per_device(): pl.pallas_call(functools.partial(exchange_kernel, n_grp, n_dom, rows, hs,...  30.3 us
    pallas_call x1, Pallas kernels, per_device(): pl.pallas_call(functools.partial(product_kernel, n_grp, n_dom, rows, hs,...  14.5 us
    reshape x1, local copies, waits for them, and re-layouts, per_device(): return summed.reshape(owned, kc, BS * BS)  2.37 us

profile of v5, /device:TPU:0, one launch (start us, length us, event | category | flops | bytes accessed | tf_op | source)
XLA Modules:
  0.0 89.5 jit_solution(16708033460018394470)
XLA Ops:
  0.0 42.4 %gather_rows.1 = (f32[24,64,512]{2,1,0:T(8,128)}, s32[12,1,128]{2,1,0:T(1,128)}, bf16[4,16,64,192]{3,2,1,0:T(8,128)(2,1)}, f32[4,8,64,64]{3,2,1,0:T(8,128)}) custom-call(s32[4]{0:T(128)} %halo.1, s32[1,8]{1,0:T(1,128)} %picked.1, s32[1,16]{1,0:T(1,128)} %owner.3, f32[4,8,4096]{2,1,0:T(8,128)} %prolong_raw.1, s32[4,8]{1,0:T(4,128)} %prolong_cols.1, ...), custom_call_target="tpu_custom_call" | custom-call | tf_op jit(solution)/shard_map/gather_rows/pallas_call | solution.py:400
  42.4 14.5 %block_products.1.packed_in = bf16[64,256,128]{2,1,0:T(8,128)(2,1)} custom-call(s32[4,16]{1,0:T(4,128)} %cols.1, s32[12,1,128]{2,1,0:T(1,128)} %get-tuple-element.9.meta, bf16[4,16,64,192]{3,2,1,0:T(8,128)(2,1)} %get-tuple-element.10.operator_in, f32[24,64,512]{2,1,0:T(8,128)} %get-tuple-element.11.table_in), custom_call_target="tpu_custom_call" | custom-call | tf_op jit(solution)/shard_map/block_products/pallas_call | solution.py:428
  56.8 30.3 %sum_rows.1 = f32[2,16,64,64]{3,2,1,0:T(8,128)} custom-call(s32[4,8]{1,0:T(4,128)} %slots.1, s32[1,16]{1,0:T(1,128)} %owner.3, s32[12,1,128]{2,1,0:T(1,128)} %get-tuple-element.9.meta, bf16[64,256,128]{2,1,0:T(8,128)(2,1)} %block_products.1.packed_in, f32[4,8,64,64]{3,2,1,0:T(8,128)} %get-tuple-element.12.prolong_in), custom_call_target="tpu_custom_call" | custom-call | tf_op jit(solution)/shard_map/sum_rows/pallas_call | solution.py:445
  87.1 2.4 %reshape.3 = f32[2,16,4096]{2,1,0:T(8,128)} reshape(f32[2,16,64,64]{3,2,1,0:T(8,128)} %sum_rows.1) | data formatting | bytes 1048576 | tf_op jit(solution)/shard_map/reshape | solution.py:464
